TPU v7x, 32 devices: a whole 2x2x4 slice. The times are simulated.
32 devices in a mesh: dp: 8 (over z, y), section: 2 (over core), tensor: 2 (over x).
Axes of the slice: x: 2, y: 2, z: 4, core: 2. Of those that a mesh axis runs over, the one named last changes fastest.
Arguments:
- tokens: bfloat16 [128, 32, 1024], P('dp'), may hold values from -6 to 6
- counts: int32 [128], replicated, may hold values from 8 to 32, as said below
- assign: int32 [128], replicated, may hold values from 0 to 127, as said below
- qkv_weight: bfloat16 [2, 1024, 3, 1024], P('section', 'dp', None, 'tensor'), may hold values from -0.9375 to 0.9375
- out_weight: bfloat16 [2, 1024, 1024], P('section', 'dp'), may hold values from -0.1875 to 0.1875
- up_weight: bfloat16 [2, 1024, 4096], P('section', 'dp', 'tensor'), may hold values from -0.1875 to 0.1875
- up_bias: bfloat16 [2, 4096], P('section', 'tensor'), may hold values from -3 to 3
- down_weight: bfloat16 [2, 4096, 1024], P('section', 'tensor', 'dp'), may hold values from -0.09375 to 0.09375
- attn_gain: bfloat16 [2, 1024], P('section'), may hold values from 0.25 to 1.75
- mlp_gain: bfloat16 [2, 1024], P('section'), may hold values from 0.25 to 1.75
- final_gain: bfloat16 [1024], replicated, may hold values from 0.25 to 1.75
Outputs:
- encoded: bfloat16 [128, 32, 1024], P('dp', 'section', 'tensor')
Inputs may be any that keep to these rules, and one draw needn't show every extreme that they name: `counts`: every count is at least 8, and in every draw some image has all 32 slots live. assign is a permutation of the images. Slot j belongs to data group j // 16, so every data group receives 16 images; within one data group's slots the images stand in increasing order. Images of data group g are tokens rows g * 16 to (g + 1) * 16 - 1. No data group hands more than 2 images to one data group (itself included), and in every draw some pair of data groups exchanges exactly 2. Every data group receives some image from the data group half the axis away.
All inputs are finite; a program needn't handle non-finite values.
Results may differ from a plain program's by a relative error of at most 0.024.
The roundings to bfloat16 on the way count: a program that leaves them out, or rounds other values in their place, can miss the bound.
Values may be sent and summed in bfloat16 or wider, within the bound.
A program may use at most 128 MiB of HBM per device.

v0:
```python
import jax
import jax.numpy as jnp
from jax import lax
from jax.sharding import PartitionSpec as P

MICRO = 4
HEAD_DIM = 64
epsilon = 1e-06


def passed_along(value, axis, by):
    size = lax.axis_size(axis)
    return lax.ppermute(value, axis, [(i, (i + by) % size) for i in range(size)])


def broadcast(value, axis, root):
    mine = lax.axis_index(axis) == root
    return lax.psum(jnp.where(mine, value, jnp.zeros_like(value)), axis)


def layer_norm(values, gain_vector):
    average = jnp.mean(values, axis=-1, keepdims=True)
    centred = values - average
    spread = jnp.mean(centred * centred, axis=-1, keepdims=True)
    return centred * lax.rsqrt(spread + epsilon) * gain_vector.astype(jnp.float32)


def attend(normed, w_merged, live_count, head_dim):
    row_count = normed.shape[0]
    merged = jnp.dot(
        normed, w_merged.reshape(w_merged.shape[0], -1), preferred_element_type=jnp.float32
    )
    merged = merged.reshape(row_count, 3, -1, head_dim)
    scores = jnp.einsum(
        "qhd,khd->hqk", merged[:, 0], merged[:, 1], precision=lax.Precision.HIGHEST
    ) * head_dim ** (-0.5)
    visible = jnp.arange(row_count) < live_count
    scores = jnp.where(visible[None, None, :], scores, -1e30)
    weights = jax.nn.softmax(scores, axis=-1)
    mixed = jnp.einsum("hqk,khd->qhd", weights, merged[:, 2], precision=lax.Precision.HIGHEST)
    return mixed.reshape(row_count, -1).astype(jnp.bfloat16)


def local(
    tokens,
    counts,
    assign,
    qkv_weight,
    out_weight,
    up_weight,
    up_bias,
    down_weight,
    attn_gain,
    mlp_gain,
    final_gain,
):
    groups = lax.axis_size("dp")
    sections = lax.axis_size("section")
    tensor_ranks = lax.axis_size("tensor")
    images_dev, block_rows, model_width = tokens.shape
    quarter = model_width // tensor_ranks
    capacity = (images_dev + groups - 1) // groups
    total_images = assign.shape[0]
    batch_images = MICRO
    batch_count = images_dev // batch_images
    my_group = lax.axis_index("dp")
    my_section = lax.axis_index("section")
    tensor_index = lax.axis_index("tensor")
    numbers = jnp.arange(total_images, dtype=jnp.int32)
    matches = (assign[:, None] == numbers[None, :]).astype(jnp.int32)
    slot_of = jnp.sum(matches * numbers[:, None], axis=0)
    target = slot_of // images_dev
    source_group = numbers // images_dev
    earlier = (
        (source_group[:, None] == source_group[None, :])
        & (target[:, None] == target[None, :])
        & (numbers[None, :] < numbers[:, None])
    )
    rank_all = jnp.sum(earlier.astype(jnp.int32), axis=1)
    send_slot = lax.dynamic_slice_in_dim(
        target * capacity + rank_all, my_group * images_dev, images_dev
    )
    buffer_slots = jnp.arange(groups * capacity, dtype=jnp.int32)
    selector = (buffer_slots[:, None] == send_slot[None, :]).astype(jnp.bfloat16)
    outgoing = jnp.einsum(
        "sl,lbd->sbd", selector, tokens, preferred_element_type=jnp.float32
    ).astype(jnp.bfloat16)
    received = lax.all_to_all(outgoing, "dp", split_axis=0, concat_axis=0, tiled=True)
    my_images = lax.dynamic_slice_in_dim(assign, my_group * images_dev, images_dev)
    chosen = (my_images[:, None] == numbers[None, :]).astype(jnp.int32)
    receive_slot = jnp.sum(chosen * (source_group * capacity + rank_all)[None, :], axis=1)
    live_counts = jnp.sum(chosen * counts[None, :], axis=1)
    picker = (buffer_slots[None, :] == receive_slot[:, None]).astype(jnp.bfloat16)
    arrived = jnp.einsum(
        "js,sbd->jbd", picker, received, preferred_element_type=jnp.float32
    ).astype(jnp.bfloat16)
    arrived_batches = arrived.reshape(batch_count, batch_images, block_rows, model_width)
    live_batches = live_counts.reshape(batch_count, batch_images)
    qkv_full, out_full, up_full, down_full = (
        lax.all_gather(qkv_weight, "dp", axis=1, tiled=True),
        lax.all_gather(out_weight, "dp", axis=1, tiled=True),
        lax.all_gather(up_weight, "dp", axis=1, tiled=True),
        lax.all_gather(down_weight, "dp", axis=2, tiled=True),
    )
    qkv_full = qkv_full[0]
    out_full = out_full[0]
    up_full = up_full[0]
    down_full = down_full[0]
    bias_row = up_bias[0].astype(jnp.float32)
    gain_attn = attn_gain[0]
    gain_mlp = mlp_gain[0]
    row_numbers = jnp.arange(block_rows)
    flat_rows = batch_images * block_rows

    def advance(step_index, state):
        carried, stored = state
        current = lax.all_gather(carried, "tensor", axis=2, tiled=True)
        done_index = step_index - sections
        finishing = (my_section == 0) & (done_index >= 0)
        done_slot = jnp.clip(done_index, 0, batch_count - 1)
        finished_rows = row_numbers[None, :, None] < live_batches[done_slot][:, None, None]
        finished = jnp.where(
            finished_rows, layer_norm(current.astype(jnp.float32), final_gain), 0.0
        ).astype(jnp.bfloat16)
        stored = jnp.where(
            finishing, lax.dynamic_update_index_in_dim(stored, finished, done_slot, 0), stored
        )
        micro_index = step_index - my_section
        active = (micro_index >= 0) & (micro_index < batch_count)
        slot_index = jnp.clip(micro_index, 0, batch_count - 1)
        injected = lax.dynamic_index_in_dim(
            arrived_batches, jnp.clip(step_index, 0, batch_count - 1), 0, keepdims=False
        )
        incoming = jnp.where(my_section == 0, injected, current)
        live_now = live_batches[slot_index]

        def attention_part():
            normed = layer_norm(incoming.astype(jnp.float32), gain_attn).astype(jnp.bfloat16)
            return jax.vmap(
                lambda image_rows, live_count: attend(image_rows, qkv_full, live_count, HEAD_DIM)
            )(normed, live_now)

        def attention_spare():
            return jnp.zeros((batch_images, block_rows, quarter), jnp.bfloat16)

        head_out = lax.cond(active, attention_part, attention_spare)
        joined = lax.all_gather(head_out, "tensor", axis=2, tiled=True)

        def mlp_part():
            middle = incoming.reshape(flat_rows, model_width).astype(jnp.float32) + jnp.dot(
                joined.reshape(flat_rows, model_width), out_full, preferred_element_type=jnp.float32
            )
            normed_mlp = layer_norm(middle, gain_mlp).astype(jnp.bfloat16)
            hidden = jax.nn.gelu(
                jnp.dot(normed_mlp, up_full, preferred_element_type=jnp.float32) + bias_row,
                approximate=False,
            ).astype(jnp.bfloat16)
            return (middle, jnp.dot(hidden, down_full, preferred_element_type=jnp.float32))

        def mlp_spare():
            empty = jnp.zeros((flat_rows, model_width), jnp.float32)
            return (empty, empty)

        middle, partial_value = lax.cond(active, mlp_part, mlp_spare)
        shares = lax.psum_scatter(
            partial_value.astype(jnp.bfloat16), "tensor", scatter_dimension=1, tiled=True
        ).astype(jnp.float32)
        own_share = lax.dynamic_slice_in_dim(middle, tensor_index * quarter, quarter, 1)
        updated = (
            (own_share + shares).astype(jnp.bfloat16).reshape(batch_images, block_rows, quarter)
        )
        carried = passed_along(updated, "section", 1)
        return (carried, stored)

    initial = (
        jnp.zeros((batch_images, block_rows, quarter), jnp.bfloat16),
        jnp.zeros((batch_count, batch_images, block_rows, model_width), jnp.bfloat16),
    )
    carried, stored = lax.fori_loop(0, batch_count + sections, advance, initial)
    stored = stored.reshape(images_dev, block_rows, model_width)
    my_piece = lax.dynamic_slice_in_dim(stored, tensor_index * quarter, quarter, 2)
    spread = broadcast(my_piece, "section", 0)
    section_rows = block_rows // sections
    return lax.dynamic_slice_in_dim(spread, my_section * section_rows, section_rows, 1)


def solution(mesh):
    in_specs = (
        P("dp", None, None),
        P(),
        P(),
        P("section", "dp", None, "tensor"),
        P("section", "dp", None),
        P("section", "dp", "tensor"),
        P("section", "tensor"),
        P("section", "tensor", "dp"),
        P("section", None),
        P("section", None),
        P(),
    )
    out_specs = P("dp", "section", "tensor")
    return jax.shard_map(local, mesh=mesh, in_specs=in_specs, out_specs=out_specs, check_vma=False)
```

profile of v0, /device:TPU:0, one launch (start us, length us, event | category | flops | bytes accessed | tf_op | source)
XLA Modules:
  0.0 576.1 jit_solution(2311422766453699122)
XLA Ops:
  14.1 7.3 %all-to-all-start = ((bf16[16,32,1024]{2,1,0:T(8,128)(2,1)}), bf16[16,32,1024]{2,1,0:T(8,128)(2,1)S(1)}, u32[]{:S(2)}, u32[]{:S(2)}) async-start(bf16[16,32,1024]{2,1,0:T(8,128)(2,1)} %copy.29), calls=%async_computation.1 | async-start | bytes 2097152 | tf_op jit(solution)/shard_map/all_to_all | solution.py:88
  21.8 36.7 %all-to-all-done = bf16[16,32,1024]{2,1,0:T(8,128)(2,1)S(1)} async-done(((bf16[16,32,1024]{2,1,0:T(8,128)(2,1)}), bf16[16,32,1024]{2,1,0:T(8,128)(2,1)S(1)}, u32[]{:S(2)}, u32[]{:S(2)}) %all-to-all-start) | async-done | bytes 1048608 | tf_op jit(solution)/shard_map/all_to_all | solution.py:88
  60.9 12.2 %all-gather.7.cloned.1.call-done = bf16[1,1024,1024]{2,1,0:T(8,128)(2,1)} async-done(((bf16[1,128,1024]{2,1,0:T(8,128)(2,1)}), bf16[1,1024,1024]{2,1,0:T(8,128)(2,1)}) %all-gather.7.cloned.1.call-update) | async-done | bytes 2097168 | tf_op jit(solution)/shard_map/all_gather | solution.py:101
  73.1 63.3 %all-gather.5.cloned.1.call-done = bf16[1,1024,3,512]{1,3,2,0:T(8,128)(2,1)} async-done(((bf16[1,128,3,512]{1,3,2,0:T(8,128)(2,1)}), bf16[1,1024,3,512]{1,3,2,0:T(8,128)(2,1)}) %all-gather.5.cloned.1.call-update) | async-done | bytes 3145744 | tf_op jit(solution)/shard_map/all_gather | solution.py:100
  136.4 73.2 %all-gather.9.cloned.1.call-done = bf16[1,1024,2048]{2,1,0:T(8,128)(2,1)} async-done(((bf16[1,128,2048]{2,1,0:T(8,128)(2,1)}), bf16[1,1024,2048]{2,1,0:T(8,128)(2,1)}) %all-gather.9.cloned.1.call-update) | async-done | bytes 4194320 | tf_op jit(solution)/shard_map/all_gather | solution.py:102
  209.5 75.1 %all-gather.11.cloned.1.call-done = bf16[1,2048,1024]{2,1,0:T(8,128)(2,1)} async-done(((bf16[1,2048,128]{2,1,0:T(8,128)(2,1)}), bf16[1,2048,1024]{2,1,0:T(8,128)(2,1)}) %all-gather.11.cloned.1.call-update) | async-done | bytes 4194320 | tf_op jit(solution)/shard_map/all_gather | solution.py:103
  285.7 260.2 %while.18 = (s32[]{:T(128)}, bf16[4,32,512]{2,1,0:T(8,128)(2,1)S(1)}, bf16[4,4,32,1024]{3,2,1,0:T(8,128)(2,1)}, s32[]{:T(128)}, pred[]{:T(512)}, /*index=5*/bf16...) while((s32[]{:T(128)}, ...), condition=%wide.region_18.19_spmd.clone, body=%wide.region_4.18_spmd.clone.sunk | while | flops 1817675392 | bytes 26838016 | solution.py:179
  304.6 11.4 %conditional.7 = (f32[128,1024]{1,0:T(8,128)}, f32[128,1024]{1,0:T(8,128)S(1)}) conditional(s32[]{:T(128)} %convert_element_type.220, () %tuple.72, (bf16[4,32,1024]{2,1,0:T(8,128)(2,1)S(1)}, bf16[4,32,1024]{2,1,0:T(8,128)(2,1)S(1)}, bf16[1024,1024]{1,0:T(8,128)(2,1)}, bf16[1024]{0:T(1024)(128)(2,1)S(1)}, bf16[1024,2048]{1,0:T(8,128)(2,1)}, ...), branch_computations={%region_11.11_spmd, %region_12.14_spmd} | conditional | flops 1360790656 | bytes 13130256 | solution.py:164
  308.7 7.3 %fusion.29 = f32[128,1024]{1,0:T(8,128)S(1)} fusion(bf16[2048,1024]{1,0:T(8,128)(2,1)} %get-tuple-element.436, bf16[1024,2048]{1,0:T(8,128)(2,1)} %get-tuple-element.434, f32[2048]{0:T(1024)S(1)} %get-tuple-element.435, f32[128,1024]{1,0:T(8,128)} %get-tuple-element.704, f32[1024]{0:T(1024)S(1)} %convert_element_type.116, f32[128]{0:T(128)S(1)} %add_rsqrt_fusion.1, ...), kind=kOutput, calls=%fused_computation.50 | convolution fusion | flops 1091567616 | bytes 9450496 | tf_op jit(solution)/shard_map/while/body/eval_jaxpr/cond/branch_1_fun/dot_general | solution.py:158
  317.3 9.9 %reduce-scatter.2.cloned.1.call-done = bf16[128,512]{1,0:T(8,128)(2,1)} async-done(((bf16[128,1024]{1,0:T(8,128)(2,1)}), bf16[128,512]{1,0:T(8,128)(2,1)}) %reduce-scatter.2.cloned.1.call-update) | async-done | bytes 131088 | tf_op jit(solution)/shard_map/while/body/eval_jaxpr/reduce_scatter | solution.py:165
  330.3 6.5 %all_gather.40 = bf16[4,32,1024]{2,1,0:T(8,128)(2,1)S(1)} all-gather(bf16[4,32,512]{2,1,0:T(8,128)(2,1)S(1)} %get-tuple-element.728), channel_id=1, replica_groups=mesh['dp'=8,'section'=2,'tensor'=2] {'tensor'}, dimensions={2}, use_global_device_ids=true | all-gather | bytes 393216 | tf_op jit(solution)/shard_map/while/body/eval_jaxpr/all_gather | solution.py:117
  350.0 11.4 %conditional.7 = (f32[128,1024]{1,0:T(8,128)}, f32[128,1024]{1,0:T(8,128)S(1)}) conditional(s32[]{:T(128)} %convert_element_type.220, () %tuple.72, (bf16[4,32,1024]{2,1,0:T(8,128)(2,1)S(1)}, bf16[4,32,1024]{2,1,0:T(8,128)(2,1)S(1)}, bf16[1024,1024]{1,0:T(8,128)(2,1)}, bf16[1024]{0:T(1024)(128)(2,1)S(1)}, bf16[1024,2048]{1,0:T(8,128)(2,1)}, ...), branch_computations={%region_11.11_spmd, %region_12.14_spmd} | conditional | flops 1360790656 | bytes 13130256 | solution.py:164
  354.1 7.3 %fusion.29 = f32[128,1024]{1,0:T(8,128)S(1)} fusion(bf16[2048,1024]{1,0:T(8,128)(2,1)} %get-tuple-element.436, bf16[1024,2048]{1,0:T(8,128)(2,1)} %get-tuple-element.434, f32[2048]{0:T(1024)S(1)} %get-tuple-element.435, f32[128,1024]{1,0:T(8,128)} %get-tuple-element.704, f32[1024]{0:T(1024)S(1)} %convert_element_type.116, f32[128]{0:T(128)S(1)} %add_rsqrt_fusion.1, ...), kind=kOutput, calls=%fused_computation.50 | convolution fusion | flops 1091567616 | bytes 9450496 | tf_op jit(solution)/shard_map/while/body/eval_jaxpr/cond/branch_1_fun/dot_general | solution.py:158
  362.6 11.5 %reduce-scatter.2.cloned.1.call-done = bf16[128,512]{1,0:T(8,128)(2,1)} async-done(((bf16[128,1024]{1,0:T(8,128)(2,1)}), bf16[128,512]{1,0:T(8,128)(2,1)}) %reduce-scatter.2.cloned.1.call-update) | async-done | bytes 131088 | tf_op jit(solution)/shard_map/while/body/eval_jaxpr/reduce_scatter | solution.py:165
  377.2 6.5 %all_gather.40 = bf16[4,32,1024]{2,1,0:T(8,128)(2,1)S(1)} all-gather(bf16[4,32,512]{2,1,0:T(8,128)(2,1)S(1)} %get-tuple-element.728), channel_id=1, replica_groups=mesh['dp'=8,'section'=2,'tensor'=2] {'tensor'}, dimensions={2}, use_global_device_ids=true | all-gather | bytes 393216 | tf_op jit(solution)/shard_map/while/body/eval_jaxpr/all_gather | solution.py:117
  396.9 11.4 %conditional.7 = (f32[128,1024]{1,0:T(8,128)}, f32[128,1024]{1,0:T(8,128)S(1)}) conditional(s32[]{:T(128)} %convert_element_type.220, () %tuple.72, (bf16[4,32,1024]{2,1,0:T(8,128)(2,1)S(1)}, bf16[4,32,1024]{2,1,0:T(8,128)(2,1)S(1)}, bf16[1024,1024]{1,0:T(8,128)(2,1)}, bf16[1024]{0:T(1024)(128)(2,1)S(1)}, bf16[1024,2048]{1,0:T(8,128)(2,1)}, ...), branch_computations={%region_11.11_spmd, %region_12.14_spmd} | conditional | flops 1360790656 | bytes 13130256 | solution.py:164
  401.0 7.3 %fusion.29 = f32[128,1024]{1,0:T(8,128)S(1)} fusion(bf16[2048,1024]{1,0:T(8,128)(2,1)} %get-tuple-element.436, bf16[1024,2048]{1,0:T(8,128)(2,1)} %get-tuple-element.434, f32[2048]{0:T(1024)S(1)} %get-tuple-element.435, f32[128,1024]{1,0:T(8,128)} %get-tuple-element.704, f32[1024]{0:T(1024)S(1)} %convert_element_type.116, f32[128]{0:T(128)S(1)} %add_rsqrt_fusion.1, ...), kind=kOutput, calls=%fused_computation.50 | convolution fusion | flops 1091567616 | bytes 9450496 | tf_op jit(solution)/shard_map/while/body/eval_jaxpr/cond/branch_1_fun/dot_general | solution.py:158
  409.6 11.5 %reduce-scatter.2.cloned.1.call-done = bf16[128,512]{1,0:T(8,128)(2,1)} async-done(((bf16[128,1024]{1,0:T(8,128)(2,1)}), bf16[128,512]{1,0:T(8,128)(2,1)}) %reduce-scatter.2.cloned.1.call-update) | async-done | bytes 131088 | tf_op jit(solution)/shard_map/while/body/eval_jaxpr/reduce_scatter | solution.py:165
  443.9 11.4 %conditional.7 = (f32[128,1024]{1,0:T(8,128)}, f32[128,1024]{1,0:T(8,128)S(1)}) conditional(s32[]{:T(128)} %convert_element_type.220, () %tuple.72, (bf16[4,32,1024]{2,1,0:T(8,128)(2,1)S(1)}, bf16[4,32,1024]{2,1,0:T(8,128)(2,1)S(1)}, bf16[1024,1024]{1,0:T(8,128)(2,1)}, bf16[1024]{0:T(1024)(128)(2,1)S(1)}, bf16[1024,2048]{1,0:T(8,128)(2,1)}, ...), branch_computations={%region_11.11_spmd, %region_12.14_spmd} | conditional | flops 1360790656 | bytes 13130256 | solution.py:164
  448.0 7.3 %fusion.29 = f32[128,1024]{1,0:T(8,128)S(1)} fusion(bf16[2048,1024]{1,0:T(8,128)(2,1)} %get-tuple-element.436, bf16[1024,2048]{1,0:T(8,128)(2,1)} %get-tuple-element.434, f32[2048]{0:T(1024)S(1)} %get-tuple-element.435, f32[128,1024]{1,0:T(8,128)} %get-tuple-element.704, f32[1024]{0:T(1024)S(1)} %convert_element_type.116, f32[128]{0:T(128)S(1)} %add_rsqrt_fusion.1, ...), kind=kOutput, calls=%fused_computation.50 | convolution fusion | flops 1091567616 | bytes 9450496 | tf_op jit(solution)/shard_map/while/body/eval_jaxpr/cond/branch_1_fun/dot_general | solution.py:158
  456.5 11.5 %reduce-scatter.2.cloned.1.call-done = bf16[128,512]{1,0:T(8,128)(2,1)} async-done(((bf16[128,1024]{1,0:T(8,128)(2,1)}), bf16[128,512]{1,0:T(8,128)(2,1)}) %reduce-scatter.2.cloned.1.call-update) | async-done | bytes 131088 | tf_op jit(solution)/shard_map/while/body/eval_jaxpr/reduce_scatter | solution.py:165
  486.4 26.6 %reduce-scatter.2.cloned.1.call-done = bf16[128,512]{1,0:T(8,128)(2,1)} async-done(((bf16[128,1024]{1,0:T(8,128)(2,1)}), bf16[128,512]{1,0:T(8,128)(2,1)}) %reduce-scatter.2.cloned.1.call-update) | async-done | bytes 131088 | tf_op jit(solution)/shard_map/while/body/eval_jaxpr/reduce_scatter | solution.py:165
  531.5 11.4 %reduce-scatter.2.cloned.1.call-done = bf16[128,512]{1,0:T(8,128)(2,1)} async-done(((bf16[128,1024]{1,0:T(8,128)(2,1)}), bf16[128,512]{1,0:T(8,128)(2,1)}) %reduce-scatter.2.cloned.1.call-update) | async-done | bytes 131088 | tf_op jit(solution)/shard_map/while/body/eval_jaxpr/reduce_scatter | solution.py:165
  547.9 20.0 %all-reduce.2.cloned.1.call-done = bf16[16,32,512]{2,1,0:T(8,128)(2,1)} async-done(((bf16[16,32,512]{2,1,0:T(8,128)(2,1)}), bf16[16,32,512]{2,1,0:T(8,128)(2,1)}) %all-reduce.2.cloned.1.call-update) | async-done | bytes 524304 | tf_op jit(solution)/shard_map/psum | solution.py:18
  (230 shorter events, 177.6 us)
Async XLA Ops:
  6.5 66.6 %all-gather.7.cloned.1.call-start = ((), (), s32[]{:S(2)}) async-start(), calls=%async_computation.3 | async-start | bytes 2359296 | tf_op jit(solution)/shard_map/all_gather | solution.py:101
  7.3 129.1 %all-gather.5.cloned.1.call-start = ((), (), s32[]{:S(2)}) async-start(), calls=%async_computation.2 | async-start | bytes 3538944 | tf_op jit(solution)/shard_map/all_gather | solution.py:100
  9.3 200.3 %all-gather.9.cloned.1.call-start = ((), (), s32[]{:S(2)}) async-start(), calls=%async_computation.4 | async-start | bytes 4718592 | tf_op jit(solution)/shard_map/all_gather | solution.py:102
  10.0 274.6 %all-gather.11.cloned.1.call-start = ((), (), s32[]{:S(2)}) async-start(), calls=%async_computation.5 | async-start | bytes 4718592 | tf_op jit(solution)/shard_map/all_gather | solution.py:103
  11.6 9.7 %copy-start.6 = (s32[128]{0:T(128)S(1)}, s32[128]{0:T(128)}, u32[]{:S(2)}) copy-start(s32[128]{0:T(128)} %param.19) | copy-start | bytes 1540
  11.7 9.8 %copy-start.5 = (s32[128]{0:T(128)S(1)}, s32[128]{0:T(128)}, u32[]{:S(2)}) copy-start(s32[128]{0:T(128)} %param.18) | copy-start | bytes 1540
  11.7 10.1 %copy-start.2 = (bf16[1,2048]{1,0:T(2,128)(2,1)S(1)}, bf16[1,2048]{1,0:T(2,128)(2,1)}, u32[]{:S(2)}) copy-start(bf16[1,2048]{1,0:T(2,128)(2,1)} %param.23) | copy-start | bytes 12292
  11.7 10.1 %copy-start.3 = (bf16[1,1024]{1,0:T(2,128)(2,1)S(1)}, bf16[1,1024]{1,0:T(2,128)(2,1)}, u32[]{:S(2)}) copy-start(bf16[1,1024]{1,0:T(2,128)(2,1)} %param.25) | copy-start | bytes 6148
  11.7 10.1 %copy-start.4 = (bf16[1,1024]{1,0:T(2,128)(2,1)S(1)}, bf16[1,1024]{1,0:T(2,128)(2,1)}, u32[]{:S(2)}) copy-start(bf16[1,1024]{1,0:T(2,128)(2,1)} %param.26) | copy-start | bytes 6148
  14.1 44.5 %all-to-all-start = ((bf16[16,32,1024]{2,1,0:T(8,128)(2,1)}), bf16[16,32,1024]{2,1,0:T(8,128)(2,1)S(1)}, u32[]{:S(2)}, u32[]{:S(2)}) async-start(bf16[16,32,1024]{2,1,0:T(8,128)(2,1)} %copy.29), calls=%async_computation.1 | async-start | bytes 2097152 | tf_op jit(solution)/shard_map/all_to_all | solution.py:88
  21.4 264.4 %copy-start.1 = (bf16[1024]{0:T(1024)(128)(2,1)S(1)}, bf16[1024]{0:T(1024)(128)(2,1)}, u32[]{:S(2)}) copy-start(bf16[1024]{0:T(1024)(128)(2,1)} %param.27) | copy-start | bytes 6148
  285.8 41.4 %reduce-scatter.2.cloned.1.call-start = ((), (), s32[]{:S(2)}) async-start(), calls=%async_computation.7 | async-start | bytes 393216 | tf_op jit(solution)/shard_map/while/body/eval_jaxpr/reduce_scatter | solution.py:165
  328.2 2.0 collective-permute-start
  330.3 43.9 %reduce-scatter.2.cloned.1.call-start = ((), (), s32[]{:S(2)}) async-start(), calls=%async_computation.7 | async-start | bytes 393216 | tf_op jit(solution)/shard_map/while/body/eval_jaxpr/reduce_scatter | solution.py:165
  375.2 2.0 collective-permute-start
  377.2 43.9 %reduce-scatter.2.cloned.1.call-start = ((), (), s32[]{:S(2)}) async-start(), calls=%async_computation.7 | async-start | bytes 393216 | tf_op jit(solution)/shard_map/while/body/eval_jaxpr/reduce_scatter | solution.py:165
  422.1 2.0 collective-permute-start
  424.1 43.9 %reduce-scatter.2.cloned.1.call-start = ((), (), s32[]{:S(2)}) async-start(), calls=%async_computation.7 | async-start | bytes 393216 | tf_op jit(solution)/shard_map/while/body/eval_jaxpr/reduce_scatter | solution.py:165
  469.0 2.0 collective-permute-start
  471.1 41.9 %reduce-scatter.2.cloned.1.call-start = ((), (), s32[]{:S(2)}) async-start(), calls=%async_computation.7 | async-start | bytes 393216 | tf_op jit(solution)/shard_map/while/body/eval_jaxpr/reduce_scatter | solution.py:165
  514.1 2.0 collective-permute-start
  516.1 26.8 %reduce-scatter.2.cloned.1.call-start = ((), (), s32[]{:S(2)}) async-start(), calls=%async_computation.7 | async-start | bytes 393216 | tf_op jit(solution)/shard_map/while/body/eval_jaxpr/reduce_scatter | solution.py:165
  544.0 2.0 collective-permute-start
  546.0 21.9 %all-reduce.2.cloned.1.call-start = ((), (), s32[]{:S(2)}) async-start(), calls=%async_computation.6 | async-start | bytes 1048576 | tf_op jit(solution)/shard_map/psum | solution.py:18
  (1 other events, 5.1 us)
Sparse Core Ops, SparseCore 0:
  9.5 63.6 all-gather.6
  75.2 61.1 all-gather.4
  138.5 70.9 all-gather.8
  211.4 73.1 all-gather.10
  316.9 10.2 reduce-scatter.1
  362.3 11.7 reduce-scatter.1
  409.2 11.7 reduce-scatter.1
  456.2 11.7 reduce-scatter.1
  486.1 26.8 reduce-scatter.1
  531.1 11.7 reduce-scatter.1
  549.1 18.7 all-reduce.1
where the time goes:
time: 577 us; the launch traced here: 576 us
  waiting for transfers between devices  365 us (63%)
  blocking collectives  72.4 us (13%)
  matrix products  64.4 us (11%)
  other arithmetic  41.1 us (7%)
  between operations  13.2 us (2%)
  local copies, waits for them, and re-layouts  11.3 us (2%)
  starting transfers between devices  7.91 us (1%)
    reduce_scatter x6, waiting for transfers between devices, advance(): lax.psum_scatter(partial_value.astype(jnp.bfloat16), 'tensor', scatter_di...  82.3 us
    all_gather x1, waiting for transfers between devices, local(): lax.all_gather(down_weight, 'dp', axis=2, tiled=True)  75.1 us
    all_gather x1, waiting for transfers between devices, local(): lax.all_gather(up_weight, 'dp', axis=1, tiled=True)  73.2 us
    all_gather x1, waiting for transfers between devices, local(): lax.all_gather(qkv_weight, 'dp', axis=1, tiled=True)  63.3 us
    all_gather x6, blocking collectives, advance(): current = lax.all_gather(carried, 'tensor', axis=2, tiled=True)  38.3 us
    all_to_all x1, waiting for transfers between devices, local(): lax.all_to_all(outgoing, 'dp', split_axis=0, concat_axis=0, tiled=True)  36.7 us
    all_gather x6, blocking collectives, advance(): joined = lax.all_gather(head_out, 'tensor', axis=2, tiled=True)  34 us
    dot_general x4, matrix products, mlp_part(): jnp.dot(hidden, down_full, preferred_element_type=jnp.float32)  29.2 us
  transfers between devices with their start and end apart: 18, of which 12 were waited for; matrix products, arithmetic and copies ran while one was open for 4% of the time, Pallas kernels for 0%

commit v1 on v0

--- a/solution.py
+++ b/solution.py
@@ -6,6 +6,17 @@
 MICRO = 4
 HEAD_DIM = 64
 epsilon = 1e-06
+
+
+def collect(x, axis, dim):
+    ways = lax.axis_size(axis)
+    pieces = [x]
+    for far in range(1, ways):
+        pieces.append(
+            lax.ppermute(pieces[far - 1], axis, [(d, (d - 1) % ways) for d in range(ways)])
+        )
+    line = jnp.concatenate(pieces, axis=dim)
+    return jnp.roll(line, lax.axis_index(axis) * x.shape[dim], axis=dim)
 
 
 def passed_along(value, axis, by):
@@ -97,7 +108,7 @@
     arrived_batches = arrived.reshape(batch_count, batch_images, block_rows, model_width)
     live_batches = live_counts.reshape(batch_count, batch_images)
     qkv_full, out_full, up_full, down_full = (
-        lax.all_gather(qkv_weight, "dp", axis=1, tiled=True),
+        collect(qkv_weight, "dp", 1),
         lax.all_gather(out_weight, "dp", axis=1, tiled=True),
         lax.all_gather(up_weight, "dp", axis=1, tiled=True),
         lax.all_gather(down_weight, "dp", axis=2, tiled=True),

time: 577 us -> 558 us (0.967)
  waiting for transfers between devices: 365 us -> 285 us
  starting transfers between devices: 7.91 us -> 41.5 us
  local copies, waits for them, and re-layouts: 11.3 us -> 37.3 us
    ppermute x0 -> x7, waiting for transfers between devices: none -> 71.8 us  [collect(): lax.ppermute(pieces[far - 1], axis, [(d, (d - 1) % ways) for d in range(w...]
    all_gather x1 -> x0, waiting for transfers between devices: 63.3 us -> none  [local(): lax.all_gather(qkv_weight, 'dp', axis=1, tiled=True)]
    all_gather x1, waiting for transfers between devices: 73.2 us -> 34.2 us  [local(): lax.all_gather(up_weight, 'dp', axis=1, tiled=True)]
    ppermute x0 -> x7, starting transfers between devices: none -> 37.4 us  [collect(): lax.ppermute(pieces[far - 1], axis, [(d, (d - 1) % ways) for d in range(w...]
    all_to_all x1, waiting for transfers between devices: 36.7 us -> 0.01 us  [local(): lax.all_to_all(outgoing, 'dp', split_axis=0, concat_axis=0, tiled=True)]
    unnamed x16 -> x35, local copies, waits for them, and re-layouts: 3.53 us -> 23.7 us
    all_gather x1, waiting for transfers between devices: 12.2 us -> 0.01 us  [local(): lax.all_gather(out_weight, 'dp', axis=1, tiled=True)]
  transfers between devices with their start and end apart: 18 -> 24, of which waited for: 12 -> 16; matrix products, arithmetic and copies ran while one was open for 4% -> 9% of each run, Pallas kernels for 0% -> 0%
where the time goes in v1:
time: 558 us; the launch traced here: 557 us
  waiting for transfers between devices  285 us (51%)
  blocking collectives  72.4 us (13%)
  matrix products  64.5 us (12%)
  starting transfers between devices  41.5 us (7%)
  other arithmetic  40.9 us (7%)
  local copies, waits for them, and re-layouts  37.3 us (7%)
  between operations  13.6 us (2%)
    reduce_scatter x6, waiting for transfers between devices, advance(): lax.psum_scatter(partial_value.astype(jnp.bfloat16), 'tensor', scatter_di...  82.3 us
    all_gather x1, waiting for transfers between devices, local(): lax.all_gather(down_weight, 'dp', axis=2, tiled=True)  75.3 us
    ppermute x7, waiting for transfers between devices, collect(): lax.ppermute(pieces[far - 1], axis, [(d, (d - 1) % ways) for d in range(w...  71.8 us
    all_gather x6, blocking collectives, advance(): current = lax.all_gather(carried, 'tensor', axis=2, tiled=True)  38.3 us
    ppermute x7, starting transfers between devices, collect(): lax.ppermute(pieces[far - 1], axis, [(d, (d - 1) % ways) for d in range(w...  37.4 us
    all_gather x1, waiting for transfers between devices, local(): lax.all_gather(up_weight, 'dp', axis=1, tiled=True)  34.2 us
    all_gather x6, blocking collectives, advance(): joined = lax.all_gather(head_out, 'tensor', axis=2, tiled=True)  34 us
    dot_general x4, matrix products, mlp_part(): jnp.dot(hidden, down_full, preferred_element_type=jnp.float32)  29.2 us
  transfers between devices with their start and end apart: 24, of which 16 were waited for; matrix products, arithmetic and copies ran while one was open for 9% of the time, Pallas kernels for 0%

profile of v1, /device:TPU:0, one launch (start us, length us, event | category | flops | bytes accessed | tf_op | source)
XLA Modules:
  0.0 556.6 jit_solution(9524280476235672162)
XLA Ops:
  17.1 12.0 %collective-permute-done.1 = bf16[1,128,3,512]{1,3,2,0:T(8,128)(2,1)S(1)} collective-permute-done((bf16[1,128,3,512]{1,3,2,0:T(8,128)(2,1)S(1)}, bf16[1,128,3,512]{1,3,2,0:T(8,128)(2,1)S(1)}, u32[]{:S(2)}, u32[]{:S(2)}) %collective-permute-start.1) | collective-permute-done | bytes 393248 | tf_op jit(solution)/shard_map/ppermute | solution.py:16
  49.0 34.4 %collective-permute-done.3 = bf16[1,128,3,512]{1,3,2,0:T(8,128)(2,1)S(1)} collective-permute-done((bf16[1,128,3,512]{1,3,2,0:T(8,128)(2,1)S(1)}, bf16[1,128,3,512]{1,3,2,0:T(8,128)(2,1)S(1)}, u32[]{:S(2)}, u32[]{:S(2)}) %collective-permute-start.3) | collective-permute-done | bytes 393248 | tf_op jit(solution)/shard_map/ppermute | solution.py:16
  131.3 8.1 %collective-permute-done.7 = bf16[1,128,3,512]{1,3,2,0:T(8,128)(2,1)} collective-permute-done((bf16[1,128,3,512]{1,3,2,0:T(8,128)(2,1)}, bf16[1,128,3,512]{1,3,2,0:T(8,128)(2,1)}, u32[]{:S(2)}, u32[]{:S(2)}) %collective-permute-start.7) | collective-permute-done | bytes 393248 | tf_op jit(solution)/shard_map/ppermute | solution.py:16
  155.7 34.2 %all-gather.6.cloned.1.call-done = bf16[1,1024,2048]{2,1,0:T(8,128)(2,1)} async-done(((bf16[1,128,2048]{2,1,0:T(8,128)(2,1)}), bf16[1,1024,2048]{2,1,0:T(8,128)(2,1)}) %all-gather.6.cloned.1.call-update) | async-done | bytes 4194320 | tf_op jit(solution)/shard_map/all_gather | solution.py:113
  189.9 75.3 %all-gather.8.cloned.1.call-done = bf16[1,2048,1024]{2,1,0:T(8,128)(2,1)} async-done(((bf16[1,2048,128]{2,1,0:T(8,128)(2,1)}), bf16[1,2048,1024]{2,1,0:T(8,128)(2,1)}) %all-gather.8.cloned.1.call-update) | async-done | bytes 4194320 | tf_op jit(solution)/shard_map/all_gather | solution.py:114
  266.3 260.2 %while.18 = (s32[]{:T(128)}, bf16[4,32,512]{2,1,0:T(8,128)(2,1)S(1)}, bf16[4,4,32,1024]{3,2,1,0:T(8,128)(2,1)}, s32[]{:T(128)}, pred[]{:T(512)}, /*index=5*/bf16...) while((s32[]{:T(128)}, ...), condition=%wide.region_18.19_spmd.clone, body=%wide.region_4.18_spmd.clone.sunk | while | flops 1817675392 | bytes 26838016 | solution.py:190
  285.1 11.4 %conditional.7 = (f32[128,1024]{1,0:T(8,128)}, f32[128,1024]{1,0:T(8,128)S(1)}) conditional(s32[]{:T(128)} %convert_element_type.220, () %tuple.72, (bf16[4,32,1024]{2,1,0:T(8,128)(2,1)S(1)}, bf16[4,32,1024]{2,1,0:T(8,128)(2,1)S(1)}, bf16[1024,1024]{1,0:T(8,128)(2,1)}, bf16[1024]{0:T(1024)(128)(2,1)S(1)}, bf16[1024,2048]{1,0:T(8,128)(2,1)}, ...), branch_computations={%region_11.11_spmd, %region_12.14_spmd} | conditional | flops 1360790656 | bytes 13130256 | solution.py:175
  289.2 7.3 %fusion.29 = f32[128,1024]{1,0:T(8,128)S(1)} fusion(bf16[2048,1024]{1,0:T(8,128)(2,1)} %get-tuple-element.436, bf16[1024,2048]{1,0:T(8,128)(2,1)} %get-tuple-element.434, f32[2048]{0:T(1024)S(1)} %get-tuple-element.435, f32[128,1024]{1,0:T(8,128)} %get-tuple-element.704, f32[1024]{0:T(1024)S(1)} %convert_element_type.116, f32[128]{0:T(128)S(1)} %add_rsqrt_fusion.1, ...), kind=kOutput, calls=%fused_computation.50 | convolution fusion | flops 1091567616 | bytes 9450496 | tf_op jit(solution)/shard_map/while/body/eval_jaxpr/cond/branch_1_fun/dot_general | solution.py:169
  297.8 9.9 %reduce-scatter.2.cloned.1.call-done = bf16[128,512]{1,0:T(8,128)(2,1)} async-done(((bf16[128,1024]{1,0:T(8,128)(2,1)}), bf16[128,512]{1,0:T(8,128)(2,1)}) %reduce-scatter.2.cloned.1.call-update) | async-done | bytes 131088 | tf_op jit(solution)/shard_map/while/body/eval_jaxpr/reduce_scatter | solution.py:176
  310.8 6.5 %all_gather.36 = bf16[4,32,1024]{2,1,0:T(8,128)(2,1)S(1)} all-gather(bf16[4,32,512]{2,1,0:T(8,128)(2,1)S(1)} %get-tuple-element.728), channel_id=1, replica_groups=mesh['dp'=8,'section'=2,'tensor'=2] {'tensor'}, dimensions={2}, use_global_device_ids=true | all-gather | bytes 393216 | tf_op jit(solution)/shard_map/while/body/eval_jaxpr/all_gather | solution.py:128
  330.5 11.4 %conditional.7 = (f32[128,1024]{1,0:T(8,128)}, f32[128,1024]{1,0:T(8,128)S(1)}) conditional(s32[]{:T(128)} %convert_element_type.220, () %tuple.72, (bf16[4,32,1024]{2,1,0:T(8,128)(2,1)S(1)}, bf16[4,32,1024]{2,1,0:T(8,128)(2,1)S(1)}, bf16[1024,1024]{1,0:T(8,128)(2,1)}, bf16[1024]{0:T(1024)(128)(2,1)S(1)}, bf16[1024,2048]{1,0:T(8,128)(2,1)}, ...), branch_computations={%region_11.11_spmd, %region_12.14_spmd} | conditional | flops 1360790656 | bytes 13130256 | solution.py:175
  334.7 7.3 %fusion.29 = f32[128,1024]{1,0:T(8,128)S(1)} fusion(bf16[2048,1024]{1,0:T(8,128)(2,1)} %get-tuple-element.436, bf16[1024,2048]{1,0:T(8,128)(2,1)} %get-tuple-element.434, f32[2048]{0:T(1024)S(1)} %get-tuple-element.435, f32[128,1024]{1,0:T(8,128)} %get-tuple-element.704, f32[1024]{0:T(1024)S(1)} %convert_element_type.116, f32[128]{0:T(128)S(1)} %add_rsqrt_fusion.1, ...), kind=kOutput, calls=%fused_computation.50 | convolution fusion | flops 1091567616 | bytes 9450496 | tf_op jit(solution)/shard_map/while/body/eval_jaxpr/cond/branch_1_fun/dot_general | solution.py:169
  343.2 11.5 %reduce-scatter.2.cloned.1.call-done = bf16[128,512]{1,0:T(8,128)(2,1)} async-done(((bf16[128,1024]{1,0:T(8,128)(2,1)}), bf16[128,512]{1,0:T(8,128)(2,1)}) %reduce-scatter.2.cloned.1.call-update) | async-done | bytes 131088 | tf_op jit(solution)/shard_map/while/body/eval_jaxpr/reduce_scatter | solution.py:176
  357.7 6.5 %all_gather.36 = bf16[4,32,1024]{2,1,0:T(8,128)(2,1)S(1)} all-gather(bf16[4,32,512]{2,1,0:T(8,128)(2,1)S(1)} %get-tuple-element.728), channel_id=1, replica_groups=mesh['dp'=8,'section'=2,'tensor'=2] {'tensor'}, dimensions={2}, use_global_device_ids=true | all-gather | bytes 393216 | tf_op jit(solution)/shard_map/while/body/eval_jaxpr/all_gather | solution.py:128
  377.5 11.4 %conditional.7 = (f32[128,1024]{1,0:T(8,128)}, f32[128,1024]{1,0:T(8,128)S(1)}) conditional(s32[]{:T(128)} %convert_element_type.220, () %tuple.72, (bf16[4,32,1024]{2,1,0:T(8,128)(2,1)S(1)}, bf16[4,32,1024]{2,1,0:T(8,128)(2,1)S(1)}, bf16[1024,1024]{1,0:T(8,128)(2,1)}, bf16[1024]{0:T(1024)(128)(2,1)S(1)}, bf16[1024,2048]{1,0:T(8,128)(2,1)}, ...), branch_computations={%region_11.11_spmd, %region_12.14_spmd} | conditional | flops 1360790656 | bytes 13130256 | solution.py:175
  381.6 7.3 %fusion.29 = f32[128,1024]{1,0:T(8,128)S(1)} fusion(bf16[2048,1024]{1,0:T(8,128)(2,1)} %get-tuple-element.436, bf16[1024,2048]{1,0:T(8,128)(2,1)} %get-tuple-element.434, f32[2048]{0:T(1024)S(1)} %get-tuple-element.435, f32[128,1024]{1,0:T(8,128)} %get-tuple-element.704, f32[1024]{0:T(1024)S(1)} %convert_element_type.116, f32[128]{0:T(128)S(1)} %add_rsqrt_fusion.1, ...), kind=kOutput, calls=%fused_computation.50 | convolution fusion | flops 1091567616 | bytes 9450496 | tf_op jit(solution)/shard_map/while/body/eval_jaxpr/cond/branch_1_fun/dot_general | solution.py:169
  390.1 11.5 %reduce-scatter.2.cloned.1.call-done = bf16[128,512]{1,0:T(8,128)(2,1)} async-done(((bf16[128,1024]{1,0:T(8,128)(2,1)}), bf16[128,512]{1,0:T(8,128)(2,1)}) %reduce-scatter.2.cloned.1.call-update) | async-done | bytes 131088 | tf_op jit(solution)/shard_map/while/body/eval_jaxpr/reduce_scatter | solution.py:176
  404.6 6.5 %all_gather.36 = bf16[4,32,1024]{2,1,0:T(8,128)(2,1)S(1)} all-gather(bf16[4,32,512]{2,1,0:T(8,128)(2,1)S(1)} %get-tuple-element.728), channel_id=1, replica_groups=mesh['dp'=8,'section'=2,'tensor'=2] {'tensor'}, dimensions={2}, use_global_device_ids=true | all-gather | bytes 393216 | tf_op jit(solution)/shard_map/while/body/eval_jaxpr/all_gather | solution.py:128
  424.4 11.4 %conditional.7 = (f32[128,1024]{1,0:T(8,128)}, f32[128,1024]{1,0:T(8,128)S(1)}) conditional(s32[]{:T(128)} %convert_element_type.220, () %tuple.72, (bf16[4,32,1024]{2,1,0:T(8,128)(2,1)S(1)}, bf16[4,32,1024]{2,1,0:T(8,128)(2,1)S(1)}, bf16[1024,1024]{1,0:T(8,128)(2,1)}, bf16[1024]{0:T(1024)(128)(2,1)S(1)}, bf16[1024,2048]{1,0:T(8,128)(2,1)}, ...), branch_computations={%region_11.11_spmd, %region_12.14_spmd} | conditional | flops 1360790656 | bytes 13130256 | solution.py:175
  428.5 7.3 %fusion.29 = f32[128,1024]{1,0:T(8,128)S(1)} fusion(bf16[2048,1024]{1,0:T(8,128)(2,1)} %get-tuple-element.436, bf16[1024,2048]{1,0:T(8,128)(2,1)} %get-tuple-element.434, f32[2048]{0:T(1024)S(1)} %get-tuple-element.435, f32[128,1024]{1,0:T(8,128)} %get-tuple-element.704, f32[1024]{0:T(1024)S(1)} %convert_element_type.116, f32[128]{0:T(128)S(1)} %add_rsqrt_fusion.1, ...), kind=kOutput, calls=%fused_computation.50 | convolution fusion | flops 1091567616 | bytes 9450496 | tf_op jit(solution)/shard_map/while/body/eval_jaxpr/cond/branch_1_fun/dot_general | solution.py:169
  437.0 11.5 %reduce-scatter.2.cloned.1.call-done = bf16[128,512]{1,0:T(8,128)(2,1)} async-done(((bf16[128,1024]{1,0:T(8,128)(2,1)}), bf16[128,512]{1,0:T(8,128)(2,1)}) %reduce-scatter.2.cloned.1.call-update) | async-done | bytes 131088 | tf_op jit(solution)/shard_map/while/body/eval_jaxpr/reduce_scatter | solution.py:176
  466.9 26.6 %reduce-scatter.2.cloned.1.call-done = bf16[128,512]{1,0:T(8,128)(2,1)} async-done(((bf16[128,1024]{1,0:T(8,128)(2,1)}), bf16[128,512]{1,0:T(8,128)(2,1)}) %reduce-scatter.2.cloned.1.call-update) | async-done | bytes 131088 | tf_op jit(solution)/shard_map/while/body/eval_jaxpr/reduce_scatter | solution.py:176
  512.0 11.5 %reduce-scatter.2.cloned.1.call-done = bf16[128,512]{1,0:T(8,128)(2,1)} async-done(((bf16[128,1024]{1,0:T(8,128)(2,1)}), bf16[128,512]{1,0:T(8,128)(2,1)}) %reduce-scatter.2.cloned.1.call-update) | async-done | bytes 131088 | tf_op jit(solution)/shard_map/while/body/eval_jaxpr/reduce_scatter | solution.py:176
  528.5 19.6 %all-reduce.2.cloned.1.call-done = bf16[16,32,512]{2,1,0:T(8,128)(2,1)} async-done(((bf16[16,32,512]{2,1,0:T(8,128)(2,1)}), bf16[16,32,512]{2,1,0:T(8,128)(2,1)}) %all-reduce.2.cloned.1.call-update) | async-done | bytes 524304 | tf_op jit(solution)/shard_map/psum | solution.py:29
  (262 shorter events, 255.2 us)
Async XLA Ops:
  6.6 149.1 %all-gather.4.cloned.1.call-start = ((), (), s32[]{:S(2)}) async-start(), calls=%async_computation.2 | async-start | bytes 2359296 | tf_op jit(solution)/shard_map/all_gather | solution.py:112
  7.3 182.6 %all-gather.6.cloned.1.call-start = ((), (), s32[]{:S(2)}) async-start(), calls=%async_computation.3 | async-start | bytes 4718592 | tf_op jit(solution)/shard_map/all_gather | solution.py:113
  8.0 257.1 %all-gather.8.cloned.1.call-start = ((), (), s32[]{:S(2)}) async-start(), calls=%async_computation.4 | async-start | bytes 4718592 | tf_op jit(solution)/shard_map/all_gather | solution.py:114
  10.0 19.1 %collective-permute-start.1 = (bf16[1,128,3,512]{1,3,2,0:T(8,128)(2,1)S(1)}, bf16[1,128,3,512]{1,3,2,0:T(8,128)(2,1)S(1)}, u32[]{:S(2)}, u32[]{:S(2)}) collective-permute-start(bf16[1,128,3,512]{1,3,2,0:T(8,128)(2,1)S(1)} %copy.38), channel_id=1, source_target_pairs={{0,28},{4,0},{8,4},{12,8},{16,12},{20,16},{24,20},{28,24},{1,29},{... | collective-permute-start | bytes 1179656 | tf_op jit(solution)/shard_map/ppermute | solution.py:16
  29.1 14.7 %collective-permute-start.2 = (bf16[1,128,3,512]{1,3,2,0:T(8,128)(2,1)S(1)}, bf16[1,128,3,512]{1,3,2,0:T(8,128)(2,1)S(1)}, u32[]{:S(2)}, u32[]{:S(2)}) collective-permute-start(bf16[1,128,3,512]{1,3,2,0:T(8,128)(2,1)S(1)} %collective-permute-done.1), channel_id=1, source_target_pairs={{0,28},{4,0},{8,4},{12,8},{16,12},{20,16},{24,20},{28,24},{1,29},{... | collective-permute-start | bytes 1179656 | tf_op jit(solution)/shard_map/ppermute | solution.py:16
  36.7 88.6 %all-to-all-start = ((bf16[16,32,1024]{2,1,0:T(8,128)(2,1)}), bf16[16,32,1024]{2,1,0:T(8,128)(2,1)S(1)}, u32[]{:S(2)}, u32[]{:S(2)}) async-start(bf16[16,32,1024]{2,1,0:T(8,128)(2,1)} %copy.35), calls=%async_computation.1 | async-start | bytes 2097152 | tf_op jit(solution)/shard_map/all_to_all | solution.py:99
  43.8 39.6 %collective-permute-start.3 = (bf16[1,128,3,512]{1,3,2,0:T(8,128)(2,1)S(1)}, bf16[1,128,3,512]{1,3,2,0:T(8,128)(2,1)S(1)}, u32[]{:S(2)}, u32[]{:S(2)}) collective-permute-start(bf16[1,128,3,512]{1,3,2,0:T(8,128)(2,1)S(1)} %collective-permute-done.2), channel_id=1, source_target_pairs={{0,28},{4,0},{8,4},{12,8},{16,12},{20,16},{24,20},{28,24},{1,29},{... | collective-permute-start | bytes 1179656 | tf_op jit(solution)/shard_map/ppermute | solution.py:16
  84.2 10.5 %collective-permute-start.4 = (bf16[1,128,3,512]{1,3,2,0:T(8,128)(2,1)S(1)}, bf16[1,128,3,512]{1,3,2,0:T(8,128)(2,1)}, u32[]{:S(2)}, u32[]{:S(2)}) collective-permute-start(bf16[1,128,3,512]{1,3,2,0:T(8,128)(2,1)S(1)} %collective-permute-done.3), channel_id=1, source_target_pairs={{0,28},{4,0},{8,4},{12,8},{16,12},{20,16},{24,20},{28,24},{1,29},{... | collective-permute-start | bytes 1179656 | tf_op jit(solution)/shard_map/ppermute | solution.py:16
  94.7 12.2 %collective-permute-start.5 = (bf16[1,128,3,512]{1,3,2,0:T(8,128)(2,1)}, bf16[1,128,3,512]{1,3,2,0:T(8,128)(2,1)}, u32[]{:S(2)}, u32[]{:S(2)}) collective-permute-start(bf16[1,128,3,512]{1,3,2,0:T(8,128)(2,1)} %collective-permute-done.4), channel_id=1, source_target_pairs={{0,28},{4,0},{8,4},{12,8},{16,12},{20,16},{24,20},{28,24},{1,29},{... | collective-permute-start | bytes 1179656 | tf_op jit(solution)/shard_map/ppermute | solution.py:16
  106.9 13.2 %collective-permute-start.6 = (bf16[1,128,3,512]{1,3,2,0:T(8,128)(2,1)}, bf16[1,128,3,512]{1,3,2,0:T(8,128)(2,1)}, u32[]{:S(2)}, u32[]{:S(2)}) collective-permute-start(bf16[1,128,3,512]{1,3,2,0:T(8,128)(2,1)} %collective-permute-done.5), channel_id=1, source_target_pairs={{0,28},{4,0},{8,4},{12,8},{16,12},{20,16},{24,20},{28,24},{1,29},{... | collective-permute-start | bytes 1179656 | tf_op jit(solution)/shard_map/ppermute | solution.py:16
  120.1 19.3 %collective-permute-start.7 = (bf16[1,128,3,512]{1,3,2,0:T(8,128)(2,1)}, bf16[1,128,3,512]{1,3,2,0:T(8,128)(2,1)}, u32[]{:S(2)}, u32[]{:S(2)}) collective-permute-start(bf16[1,128,3,512]{1,3,2,0:T(8,128)(2,1)} %collective-permute-done.6), channel_id=1, source_target_pairs={{0,28},{4,0},{8,4},{12,8},{16,12},{20,16},{24,20},{28,24},{1,29},{... | collective-permute-start | bytes 1179656 | tf_op jit(solution)/shard_map/ppermute | solution.py:16
  266.3 41.4 %reduce-scatter.2.cloned.1.call-start = ((), (), s32[]{:S(2)}) async-start(), calls=%async_computation.6 | async-start | bytes 393216 | tf_op jit(solution)/shard_map/while/body/eval_jaxpr/reduce_scatter | solution.py:176
  308.8 2.0 collective-permute-start
  310.8 43.9 %reduce-scatter.2.cloned.1.call-start = ((), (), s32[]{:S(2)}) async-start(), calls=%async_computation.6 | async-start | bytes 393216 | tf_op jit(solution)/shard_map/while/body/eval_jaxpr/reduce_scatter | solution.py:176
  355.7 2.0 collective-permute-start
  357.7 43.9 %reduce-scatter.2.cloned.1.call-start = ((), (), s32[]{:S(2)}) async-start(), calls=%async_computation.6 | async-start | bytes 393216 | tf_op jit(solution)/shard_map/while/body/eval_jaxpr/reduce_scatter | solution.py:176
  402.6 2.0 collective-permute-start
  404.6 43.9 %reduce-scatter.2.cloned.1.call-start = ((), (), s32[]{:S(2)}) async-start(), calls=%async_computation.6 | async-start | bytes 393216 | tf_op jit(solution)/shard_map/while/body/eval_jaxpr/reduce_scatter | solution.py:176
  449.6 2.0 collective-permute-start
  451.6 41.9 %reduce-scatter.2.cloned.1.call-start = ((), (), s32[]{:S(2)}) async-start(), calls=%async_computation.6 | async-start | bytes 393216 | tf_op jit(solution)/shard_map/while/body/eval_jaxpr/reduce_scatter | solution.py:176
  494.5 2.0 collective-permute-start
  496.6 26.9 %reduce-scatter.2.cloned.1.call-start = ((), (), s32[]{:S(2)}) async-start(), calls=%async_computation.6 | async-start | bytes 393216 | tf_op jit(solution)/shard_map/while/body/eval_jaxpr/reduce_scatter | solution.py:176
  524.5 2.0 collective-permute-start
  526.5 21.6 %all-reduce.2.cloned.1.call-start = ((), (), s32[]{:S(2)}) async-start(), calls=%async_computation.5 | async-start | bytes 1048576 | tf_op jit(solution)/shard_map/psum | solution.py:29
  (9 other events, 639.1 us)
Sparse Core Ops, SparseCore 0:
  9.5 74.4 all-gather.3
  86.1 103.7 all-gather.5
  192.0 73.1 all-gather.7
  297.4 10.2 reduce-scatter.1
  342.9 11.7 reduce-scatter.1
  389.8 11.7 reduce-scatter.1
  436.7 11.7 reduce-scatter.1
  466.6 26.8 reduce-scatter.1
  511.6 11.7 reduce-scatter.1
  529.3 18.7 all-reduce.1
